TPU v7x, 128 devices: a whole 4x4x4 slice. The times are simulated.
128 devices in a mesh: mu: 16 (over y, z_hi, core), nu: 8 (over z_lo, x).
Axes of the slice: x: 4, y: 4, z: 4 (z_hi: 2, z_lo: 2; z = z_hi * 2 + z_lo), core: 2. Of those that a mesh axis runs over, the one named last changes fastest.
Arguments:
- earlier_vectors: float32 [1024, 1024, 512], P('mu', 'nu'), may hold values from -0.72 to 0.72
- pivot_integral_columns: float32 [1024, 1024, 256], P('mu', 'nu'), may hold values from -6 to 6
- diagonal: float32 [1024, 1024], P('mu', 'nu'), may hold values from 2 to 60
- orbitals: float32 [1024, 40], replicated, may hold values from -0.1875 to 0.1875
- pivots: int32 [256], replicated, may hold values from 0 to 1048575, as said below
Outputs:
- transformed: float32 [256, 820], P(('mu', 'nu'))
- updated_diagonal: float32 [1024, 1024], P('mu', 'nu')
Inputs may be any that keep to these rules, and one draw needn't show every extreme that they name: The pivots are distinct. The pairs held by one device (a block of 64 first by 128 second AO indices) contain at most 8 pivots, and some block contains exactly 8.
All inputs are finite; a program needn't handle non-finite values.
Results may differ from a plain program's by a relative error of at most 0.0001.
Values sent between devices are 32-bit elements; how exact they have to be, the bound alone decides.
No kernel may reach another device: no remote copies, remote signals or barrier semaphores. Data moves between devices by JAX's collectives and lax.ppermute only.
A program may use at most 128 MiB of HBM per device.

v0:
```python
import jax
import jax.numpy as jnp
import numpy as np
from jax import lax
from jax.sharding import PartitionSpec as P

precise = lax.Precision.HIGHEST


def cut_along(value, dim, length):
    dims = value.shape
    pieces = value.reshape(*dims[:dim], length, dims[dim] // length, *dims[dim + 1 :])
    return jnp.moveaxis(pieces, dim, 0)


def summed_on_arrival(value, axis, dim):
    pieces = cut_along(value, dim, lax.axis_size(axis))
    arrived = lax.all_to_all(pieces, axis, split_axis=0, concat_axis=0, tiled=True)
    return arrived.sum(axis=0)


def local(earlier_vectors, pivot_integral_columns, diagonal, orbitals, pivots):
    orbital_rows_mu, cols_nu, preceding = earlier_vectors.shape
    pivot_count = pivots.shape[0]
    ao_count, active = orbitals.shape
    size_mu = lax.axis_size("mu")
    size_nu = lax.axis_size("nu")
    index_mu = lax.axis_index("mu")
    index_nu = lax.axis_index("nu")
    pivot_mu = pivots // ao_count
    pivot_nu = pivots % ao_count
    owner_mu = pivot_mu // orbital_rows_mu
    owner_nu = pivot_nu // cols_nu
    local_row = pivot_mu % orbital_rows_mu * cols_nu + pivot_nu % cols_nu
    is_owned = (owner_mu == index_mu) & (owner_nu == index_nu)
    flat_vectors = earlier_vectors.reshape(orbital_rows_mu * cols_nu, preceding)
    flat_diag = diagonal.reshape(orbital_rows_mu * cols_nu)
    picked = jnp.take(flat_vectors, local_row, axis=0)
    picked_diag = jnp.take(flat_diag, local_row)
    masked = jnp.where(is_owned[:, None], picked, 0.0)
    masked_diag = jnp.where(is_owned, picked_diag, 0.0)
    pivot_rows, pivot_diag = lax.psum((masked, masked_diag), ("mu", "nu"))
    residual_diag = pivot_diag - jnp.sum(pivot_rows * pivot_rows, axis=1)
    scaling = lax.rsqrt(jnp.maximum(residual_diag, 1.0))
    update = lax.dot_general(flat_vectors, pivot_rows, (((1,), (1,)), ((), ())), precision=precise)
    flat_columns = pivot_integral_columns.reshape(orbital_rows_mu * cols_nu, pivot_count)
    fresh_vectors = (flat_columns - update) * scaling[None, :]
    updated_diagonal = (flat_diag - jnp.sum(fresh_vectors * fresh_vectors, axis=1)).reshape(
        orbital_rows_mu, cols_nu
    )
    basis_left_index = lax.dynamic_slice_in_dim(
        orbitals, index_mu * orbital_rows_mu, orbital_rows_mu, 0
    )
    orbit_nu = lax.dynamic_slice_in_dim(orbitals, index_nu * cols_nu, cols_nu, 0)
    fresh_blocks = fresh_vectors.reshape(orbital_rows_mu, cols_nu, pivot_count)
    half_done = jnp.einsum("mp,mnj->jpn", basis_left_index, fresh_blocks, precision=precise)
    row_index, col_index = np.tril_indices(active)
    full_done = jnp.einsum("nq,jpn->jpq", orbit_nu, half_done, precision=precise)
    pair_values = full_done[:, row_index, col_index]
    pair_count = row_index.shape[0]
    per_device = pivot_count // (size_mu * size_nu)
    split_mu = pair_values.reshape(size_mu, size_nu * per_device, pair_count)
    summed = summed_on_arrival(split_mu, "mu", 0)
    split_nu = summed.reshape(size_nu, per_device, pair_count)
    transformed = summed_on_arrival(split_nu, "nu", 0).reshape(per_device, pair_count)
    return (transformed, updated_diagonal)


def solution(mesh):
    placed = (P("mu", "nu", None), P("mu", "nu", None), P("mu", "nu"), P(), P())
    return jax.shard_map(
        local,
        mesh=mesh,
        in_specs=placed,
        out_specs=(P(("mu", "nu"), None), P("mu", "nu")),
        check_vma=False,
    )
```

profile of v0, /device:TPU:0, one launch (start us, length us, event | category | flops | bytes accessed | tf_op | source)
XLA Modules:
  0.0 257.5 jit_solution(8230308428707092736)
XLA Ops:
  7.2 0.0 all-reduce.2.cloned.1.call-start
  7.2 0.7 compare_select_fusion
  8.0 2.0 gather_fusion.1
  10.0 7.0 %gather_fusion = f32[256,512]{1,0:T(8,128)S(1)} fusion(f32[8192,512]{1,0:T(8,128)} %bitcast.34, s32[1024]{0:T(1024)S(1)} %pad_clamp_fusion), kind=kCustom, calls=%fused_computation | custom fusion | bytes 1049600 | tf_op jit(solution)/shard_map/jit(_take)/gather | solution.py:38
  17.0 0.7 select_select_fusion.1
  17.7 1.0 select_select_fusion
  18.7 8.9 %copy.20 = f32[8192,256]{0,1:T(8,128)} copy(f32[8192,256]{1,0:T(8,128)} %bitcast.36) | data formatting | bytes 16777216 | tf_op jit(solution)/shard_map/reshape | solution.py:46
  27.6 69.1 %psum.15 = f32[256]{0:T(256)S(1)} all-reduce(f32[256]{0:T(256)S(1)} %get-tuple-element.2), channel_id=1, replica_groups=mesh['mu'=16,'nu'=8] {'mu','nu'}, use_global_device_ids=true, to_apply=%region_1.2 | all-reduce | flops 256 | bytes 2048 | tf_op jit(solution)/shard_map/psum | solution.py:42
  96.8 69.2 %all-reduce.2.cloned.1.call-done = f32[256,512]{1,0:T(8,128)} async-done(((f32[256,512]{1,0:T(8,128)}), f32[256,512]{1,0:T(8,128)}) %all-reduce.2.cloned.1.call-update) | async-done | bytes 524304 | tf_op jit(solution)/shard_map/psum | solution.py:42
  166.0 1.2 multiply_reduce_fusion.1
  167.1 19.7 %multiply_reduce_fusion = (f32[8192]{0:T(1024)S(1)}, f32[8192,256]{0,1:T(8,128)S(1)}) fusion(f32[256]{0:T(256)S(1)} %maximum_rsqrt_fusion, f32[8192,256]{0,1:T(8,128)} %copy.20, f32[256,512]{1,0:T(8,128)} %all-reduce.2.cloned.1.call-done, f32[8192,512]{1,0:T(8,128)} %bitcast.35), kind=kOutput, calls=%fused_computation.6 | convolution fusion | flops 12893282304 | bytes 34112512 | tf_op jit(solution)/shard_map/dot_general | solution.py:45
  186.9 1.6 copy.21
  188.6 6.6 %fusion.5 = f32[128,256,40]{0,2,1:T(8,128)S(1)} fusion(f32[64,128,256]{1,0,2:T(8,128)S(1)} %bitcast.32, f32[1024,40]{0,1:T(8,128)S(1)} %copy-done, s32[]{:T(128)S(6)} %select_n.71), kind=kOutput, calls=%fused_computation.13 | convolution fusion | flops 1006632960 | bytes 13651972 | tf_op jit(solution)/shard_map/mp,mnj->jpn/dot_general | solution.py:56
  195.2 5.9 %fusion.2 = f32[256,40,40]{2,1,0:T(8,128)} fusion(f32[128,256,40]{0,2,1:T(8,128)S(1)} %fusion.5, f32[1024,40]{0,1:T(8,128)S(1)} %copy-done, s32[]{:T(128)S(6)} %select_n.72), kind=kOutput, calls=%fused_computation.7 | convolution fusion | flops 629145600 | bytes 6901764 | tf_op jit(solution)/shard_map/nq,jpn->jpq/dot_general | solution.py:58
  201.1 5.0 %copy.19 = f32[256,40,40]{0,2,1:T(8,128)S(1)} copy(f32[256,40,40]{2,1,0:T(8,128)} %fusion.2) | data formatting | bytes 3276800 | tf_op jit(solution)/shard_map/nq,jpn->jpq/dot_general | solution.py:58
  206.2 11.0 %gather_fusion.2 = f32[820,256]{1,0:T(8,128)S(1)} fusion(f32[256,40,40]{0,2,1:T(8,128)S(1)} %copy.19, s32[820]{0:T(1024)S(1)} %copy-done.1), kind=kCustom, calls=%fused_computation.2 | custom fusion | bytes 1685920 | tf_op jit(solution)/shard_map/gather | solution.py:59
  217.1 0.3 copy.16
  217.4 21.5 %all_to_all.10 = f32[16,1,16,820]{3,2,1,0:T(8,128)S(1)} all-to-all(f32[16,1,16,820]{3,2,1,0:T(8,128)S(1)} %bitcast.38), channel_id=1, replica_groups=mesh['mu'=16,'nu'=8] {'mu'}, dimensions={0} | all-to-all | bytes 1679360 | tf_op jit(solution)/shard_map/all_to_all | solution.py:18
  239.0 0.1 reduce_sum.39
  239.0 0.7 reshape_reshape.7
  239.7 4.0 %all-to-all-start.1 = ((f32[8,1,2,820]{3,2,1,0:T(2,128)}), f32[8,1,2,820]{3,2,1,0:T(2,128)S(1)}, u32[]{:S(2)}, u32[]{:S(2)}) async-start(f32[8,1,2,820]{3,2,1,0:T(2,128)} %reshape_reshape.7), calls=%async_computation.1 | async-start | bytes 114688 | tf_op jit(solution)/shard_map/all_to_all | solution.py:18
  243.7 0.6 bitcast_subtract_fusion
  244.4 5.7 %all-to-all-done.1 = f32[8,1,2,820]{3,2,1,0:T(2,128)S(1)} async-done(((f32[8,1,2,820]{3,2,1,0:T(2,128)}), f32[8,1,2,820]{3,2,1,0:T(2,128)S(1)}, u32[]{:S(2)}, u32[]{:S(2)}) %all-to-all-start.1) | async-done | bytes 52512 | tf_op jit(solution)/shard_map/all_to_all | solution.py:18
  250.1 0.6 reduce_sum.40
  (9 shorter events, 0.1 us)
Async XLA Ops:
  7.2 181.4 %copy-start = (f32[1024,40]{0,1:T(8,128)S(1)}, f32[1024,40]{0,1:T(8,128)}, u32[]{:S(2)}) copy-start(f32[1024,40]{0,1:T(8,128)} %param.12) | copy-start | bytes 491524
  7.2 158.8 %all-reduce.2.cloned.1.call-start = ((), (), s32[]{:S(2)}) async-start(), calls=%async_computation.2 | async-start | bytes 1048576 | tf_op jit(solution)/shard_map/psum | solution.py:42
  195.2 11.0 %copy-start.1 = (s32[820]{0:T(1024)S(1)}, s32[820]{0:T(1024)}, u32[]{:S(2)}) copy-start(s32[820]{0:T(1024)} %constant.144) | copy-start | bytes 9844
  206.1 37.6 %copy-start.2 = (f32[64,128]{1,0:T(8,128)S(1)}, f32[64,128]{1,0:T(8,128)}, u32[]{:S(2)}) copy-start(f32[64,128]{1,0:T(8,128)} %param.11) | copy-start | bytes 98308
  239.7 10.4 %all-to-all-start.1 = ((f32[8,1,2,820]{3,2,1,0:T(2,128)}), f32[8,1,2,820]{3,2,1,0:T(2,128)S(1)}, u32[]{:S(2)}, u32[]{:S(2)}) async-start(f32[8,1,2,820]{3,2,1,0:T(2,128)} %reshape_reshape.7), calls=%async_computation.1 | async-start | bytes 114688 | tf_op jit(solution)/shard_map/all_to_all | solution.py:18
Sparse Core Ops, SparseCore 0:
  18.8 147.1 all-reduce.1
where the time goes:
time: 258 us
  blocking collectives  90.7 us (35%)
  waiting for transfers between devices  74.9 us (29%)
  local copies, waits for them, and re-layouts  36.5 us (14%)
  matrix products  32.3 us (13%)
  between operations  14.1 us (5%)
  other arithmetic  4.92 us (2%)
  starting transfers between devices  4.07 us (2%)
    psum x1, waiting for transfers between devices, local(): pivot_rows, pivot_diag = lax.psum((masked, masked_diag), ('mu', 'nu'))  69.2 us
    psum x1, blocking collectives, local(): pivot_rows, pivot_diag = lax.psum((masked, masked_diag), ('mu', 'nu'))  69.1 us
    all_to_all x1, blocking collectives, summed_on_arrival(): lax.all_to_all(pieces, axis, split_axis=0, concat_axis=0, tiled=True)  21.5 us
    dot_general x1, matrix products, local(): lax.dot_general(flat_vectors, pivot_rows, (((1,), (1,)), ((), ())), preci...  19.7 us
    gather x2, local copies, waits for them, and re-layouts, local(): pair_values = full_done[:, row_index, col_index]  11.3 us
    reshape x1, local copies, waits for them, and re-layouts, local(): pivot_integral_columns.reshape(orbital_rows_mu * cols_nu, pivot_count)  8.94 us
    gather x1, local copies, waits for them, and re-layouts, local(): picked = jnp.take(flat_vectors, local_row, axis=0)  6.98 us
    dot_general x1, matrix products, local(): jnp.einsum('mp,mnj->jpn', basis_left_index, fresh_blocks, precision=precise)  6.61 us
  transfers between devices with their start and end apart: 2, of which 2 were waited for; matrix products, arithmetic and copies ran while one was open for 4% of the time, Pallas kernels for 0%

commit v1 on v0

--- a/solution.py
+++ b/solution.py
@@ -39,7 +39,7 @@
     picked_diag = jnp.take(flat_diag, local_row)
     masked = jnp.where(is_owned[:, None], picked, 0.0)
     masked_diag = jnp.where(is_owned, picked_diag, 0.0)
-    pivot_rows, pivot_diag = lax.psum((masked, masked_diag), ("mu", "nu"))
+    pivot_rows, pivot_diag = lax.psum(lax.psum((masked, masked_diag), "mu"), "nu")
     residual_diag = pivot_diag - jnp.sum(pivot_rows * pivot_rows, axis=1)
     scaling = lax.rsqrt(jnp.maximum(residual_diag, 1.0))
     update = lax.dot_general(flat_vectors, pivot_rows, (((1,), (1,)), ((), ())), precision=precise)

time: 258 us -> 331 us (1.28)
  waiting for transfers between devices: 74.9 us -> 159 us
  blocking collectives: 90.7 us -> 79.9 us
    psum x1 -> x2, waiting for transfers between devices: 69.2 us -> 154 us  [the longest x1 141 us: local(): lax.psum((masked, masked_diag), 'mu')]
    psum x1 -> x2, blocking collectives: 69.1 us -> 57.1 us  [the longest x1 38.4 us: local(): lax.psum((masked, masked_diag), 'mu')]
  transfers between devices with their start and end apart: 2 -> 3, of which waited for: 2 -> 3; matrix products, arithmetic and copies ran while one was open for 4% -> 3% of each run, Pallas kernels for 0% -> 0%
where the time goes in v1:
time: 331 us
  waiting for transfers between devices  159 us (48%)
  blocking collectives  79.9 us (24%)
  local copies, waits for them, and re-layouts  36.5 us (11%)
  matrix products  32.3 us (10%)
  between operations  14.2 us (4%)
  other arithmetic  4.83 us (1%)
  starting transfers between devices  3.43 us (1%)
    psum x1, waiting for transfers between devices, local(): lax.psum((masked, masked_diag), 'mu')  141 us
    psum x1, blocking collectives, local(): lax.psum((masked, masked_diag), 'mu')  38.4 us
    all_to_all x1, blocking collectives, summed_on_arrival(): lax.all_to_all(pieces, axis, split_axis=0, concat_axis=0, tiled=True)  22.8 us
    dot_general x1, matrix products, local(): lax.dot_general(flat_vectors, pivot_rows, (((1,), (1,)), ((), ())), preci...  19.7 us
    psum x1, blocking collectives, local(): lax.psum(lax.psum((masked, masked_diag), 'mu'), 'nu')  18.8 us
    psum x1, waiting for transfers between devices, local(): lax.psum(lax.psum((masked, masked_diag), 'mu'), 'nu')  12.4 us
    gather x2, local copies, waits for them, and re-layouts, local(): pair_values = full_done[:, row_index, col_index]  11.3 us
    reshape x1, local copies, waits for them, and re-layouts, local(): pivot_integral_columns.reshape(orbital_rows_mu * cols_nu, pivot_count)  8.94 us
  transfers between devices with their start and end apart: 3, of which 3 were waited for; matrix products, arithmetic and copies ran while one was open for 3% of the time, Pallas kernels for 0%

profile of v1, /device:TPU:0, one launch (start us, length us, event | category | flops | bytes accessed | tf_op | source)
XLA Modules:
  0.0 330.5 jit_solution(11846429407812418026)
XLA Ops:
  7.2 0.7 compare_select_fusion
  8.0 2.0 gather_fusion.1
  10.0 7.0 %gather_fusion = f32[256,512]{1,0:T(8,128)S(1)} fusion(f32[8192,512]{1,0:T(8,128)} %bitcast.34, s32[1024]{0:T(1024)S(1)} %pad_clamp_fusion), kind=kCustom, calls=%fused_computation | custom fusion | bytes 1049600 | tf_op jit(solution)/shard_map/jit(_take)/gather | solution.py:38
  17.0 0.7 select_select_fusion.1
  17.7 0.9 select_select_fusion
  18.7 141.3 %all-reduce.3.cloned.1.call-done = f32[256,512]{1,0:T(8,128)} async-done(((f32[256,512]{1,0:T(8,128)}), f32[256,512]{1,0:T(8,128)}) %all-reduce.3.cloned.1.call-update) | async-done | bytes 524304 | tf_op jit(solution)/shard_map/psum | solution.py:42
  160.0 8.9 %copy.20 = f32[8192,256]{0,1:T(8,128)} copy(f32[8192,256]{1,0:T(8,128)} %bitcast.36) | data formatting | bytes 16777216 | tf_op jit(solution)/shard_map/reshape | solution.py:46
  168.9 38.4 %psum.30 = f32[256]{0:T(256)S(1)} all-reduce(f32[256]{0:T(256)S(1)} %get-tuple-element.2), channel_id=1, replica_groups=mesh['mu'=16,'nu'=8] {'mu'}, use_global_device_ids=true, to_apply=%region_2.3 | all-reduce | flops 256 | bytes 2048 | tf_op jit(solution)/shard_map/psum | solution.py:42
  207.3 18.8 %psum.31 = f32[256]{0:T(256)S(1)} all-reduce(f32[256]{0:T(256)S(1)} %psum.30), channel_id=1, replica_groups=mesh['mu'=16,'nu'=8] {'nu'}, use_global_device_ids=true, to_apply=%region_3.4 | all-reduce | flops 256 | bytes 2048 | tf_op jit(solution)/shard_map/psum | solution.py:42
  226.1 12.4 %all-reduce.5.cloned.1.call-done = f32[256,512]{1,0:T(8,128)} async-done(((f32[256,512]{1,0:T(8,128)}), f32[256,512]{1,0:T(8,128)}) %all-reduce.5.cloned.1.call-update) | async-done | bytes 524304 | tf_op jit(solution)/shard_map/psum | solution.py:42
  238.5 1.2 multiply_reduce_fusion.1
  239.6 19.7 %multiply_reduce_fusion = (f32[8192]{0:T(1024)S(1)}, f32[8192,256]{0,1:T(8,128)S(1)}) fusion(f32[256]{0:T(256)S(1)} %maximum_rsqrt_fusion, f32[8192,256]{0,1:T(8,128)} %copy.20, f32[256,512]{1,0:T(8,128)} %all-reduce.5.cloned.1.call-done, f32[8192,512]{1,0:T(8,128)} %bitcast.35), kind=kOutput, calls=%fused_computation.6 | convolution fusion | flops 12893282304 | bytes 34112512 | tf_op jit(solution)/shard_map/dot_general | solution.py:45
  259.4 1.6 copy.21
  261.0 6.6 %fusion.5 = f32[128,256,40]{0,2,1:T(8,128)S(1)} fusion(f32[64,128,256]{1,0,2:T(8,128)S(1)} %bitcast.32, f32[1024,40]{0,1:T(8,128)S(1)} %copy-done, s32[]{:T(128)S(6)} %select_n.71), kind=kOutput, calls=%fused_computation.13 | convolution fusion | flops 1006632960 | bytes 13651972 | tf_op jit(solution)/shard_map/mp,mnj->jpn/dot_general | solution.py:56
  267.7 5.9 %fusion.2 = f32[256,40,40]{2,1,0:T(8,128)} fusion(f32[128,256,40]{0,2,1:T(8,128)S(1)} %fusion.5, f32[1024,40]{0,1:T(8,128)S(1)} %copy-done, s32[]{:T(128)S(6)} %select_n.72), kind=kOutput, calls=%fused_computation.7 | convolution fusion | flops 629145600 | bytes 6901764 | tf_op jit(solution)/shard_map/nq,jpn->jpq/dot_general | solution.py:58
  273.6 5.0 %copy.19 = f32[256,40,40]{0,2,1:T(8,128)S(1)} copy(f32[256,40,40]{2,1,0:T(8,128)} %fusion.2) | data formatting | bytes 3276800 | tf_op jit(solution)/shard_map/nq,jpn->jpq/dot_general | solution.py:58
  278.6 11.0 %gather_fusion.2 = f32[820,256]{1,0:T(8,128)S(1)} fusion(f32[256,40,40]{0,2,1:T(8,128)S(1)} %copy.19, s32[820]{0:T(1024)S(1)} %copy-done.1), kind=kCustom, calls=%fused_computation.2 | custom fusion | bytes 1685920 | tf_op jit(solution)/shard_map/gather | solution.py:59
  289.6 0.3 copy.16
  289.9 22.8 %all_to_all.10 = f32[16,1,16,820]{3,2,1,0:T(8,128)S(1)} all-to-all(f32[16,1,16,820]{3,2,1,0:T(8,128)S(1)} %bitcast.38), channel_id=1, replica_groups=mesh['mu'=16,'nu'=8] {'mu'}, dimensions={0} | all-to-all | bytes 1679360 | tf_op jit(solution)/shard_map/all_to_all | solution.py:18
  312.8 0.7 reshape_reshape.7
  313.5 3.3 %all-to-all-start.1 = ((f32[8,1,2,820]{3,2,1,0:T(2,128)}), f32[8,1,2,820]{3,2,1,0:T(2,128)S(1)}, u32[]{:S(2)}, u32[]{:S(2)}) async-start(f32[8,1,2,820]{3,2,1,0:T(2,128)} %reshape_reshape.7), calls=%async_computation.1 | async-start | bytes 114688 | tf_op jit(solution)/shard_map/all_to_all | solution.py:18
  316.8 0.6 bitcast_subtract_fusion
  317.4 5.6 %all-to-all-done.1 = f32[8,1,2,820]{3,2,1,0:T(2,128)S(1)} async-done(((f32[8,1,2,820]{3,2,1,0:T(2,128)}), f32[8,1,2,820]{3,2,1,0:T(2,128)S(1)}, u32[]{:S(2)}, u32[]{:S(2)}) %all-to-all-start.1) | async-done | bytes 52512 | tf_op jit(solution)/shard_map/all_to_all | solution.py:18
  323.1 0.6 reduce_sum.40
  (13 shorter events, 0.2 us)
Async XLA Ops:
  7.2 253.9 %copy-start = (f32[1024,40]{0,1:T(8,128)S(1)}, f32[1024,40]{0,1:T(8,128)}, u32[]{:S(2)}) copy-start(f32[1024,40]{0,1:T(8,128)} %param.12) | copy-start | bytes 491524
  7.2 152.8 %all-reduce.3.cloned.1.call-start = ((), (), s32[]{:S(2)}) async-start(), calls=%async_computation.2 | async-start | bytes 1048576 | tf_op jit(solution)/shard_map/psum | solution.py:42
  18.6 219.8 %all-reduce.5.cloned.1.call-start = ((), (), s32[]{:S(2)}) async-start(), calls=%async_computation.3 | async-start | bytes 1048576 | tf_op jit(solution)/shard_map/psum | solution.py:42
  267.7 11.0 %copy-start.1 = (s32[820]{0:T(1024)S(1)}, s32[820]{0:T(1024)}, u32[]{:S(2)}) copy-start(s32[820]{0:T(1024)} %constant.144) | copy-start | bytes 9844
  278.6 38.2 %copy-start.2 = (f32[64,128]{1,0:T(8,128)S(1)}, f32[64,128]{1,0:T(8,128)}, u32[]{:S(2)}) copy-start(f32[64,128]{1,0:T(8,128)} %param.11) | copy-start | bytes 98308
  313.5 9.6 %all-to-all-start.1 = ((f32[8,1,2,820]{3,2,1,0:T(2,128)}), f32[8,1,2,820]{3,2,1,0:T(2,128)S(1)}, u32[]{:S(2)}, u32[]{:S(2)}) async-start(f32[8,1,2,820]{3,2,1,0:T(2,128)} %reshape_reshape.7), calls=%async_computation.1 | async-start | bytes 114688 | tf_op jit(solution)/shard_map/all_to_all | solution.py:18
Sparse Core Ops, SparseCore 0:
  18.7 141.1 all-reduce.2
  162.6 75.8 all-reduce.4
